TPU v7x, 32 devices: a whole 2x2x4 slice. The times are simulated.
32 devices in a mesh: row: 8 (over y, x, core), col: 4 (over z).
Axes of the slice: x: 2, y: 2, z: 4, core: 2. Of those that a mesh axis runs over, the one named last changes fastest.
Arguments:
- left_act: bfloat16 [32, 64, 256], P(None, 'col', 'row'), may hold values from -6 to 6
- right_act: bfloat16 [32, 64, 256], P(None, 'row', 'col'), may hold values from -6 to 6
- cotangent: bfloat16 [256, 256, 128], P('row', 'col'), may hold values from -4 to 4
- weight: bfloat16 [1024, 128], replicated, may hold values from -0.1875 to 0.1875
Outputs:
- grad_left: float32 [32, 64, 256], P(None, 'col', 'row')
- grad_right: float32 [32, 64, 256], P(None, 'row', 'col')
- grad_weight: float32 [1024, 128], P('row')
All inputs are finite; a program needn't handle non-finite values.
Results may differ from a plain program's by a relative error of at most 0.0029.
Values may be sent and summed in bfloat16 or wider, within the bound.
No kernel may reach another device: no remote copies, remote signals or barrier semaphores. Data moves between devices by JAX's collectives and lax.ppermute only.
A program may use at most 128 MiB of HBM per device.

v0:
```python
import jax
import jax.numpy as jnp
from jax import lax
from jax.sharding import PartitionSpec as P

S = 64


def body(left_act, right_act, cotangent, weight):
    left = lax.all_gather(left_act, "col", axis=1, tiled=True)
    right = lax.all_gather(right_act, "row", axis=1, tiled=True)
    first, second = (cotangent.shape[0], cotangent.shape[1])
    chans = left.shape[0]
    outer = (
        jnp.einsum("csi,dsj->ijcd", left, right, preferred_element_type=jnp.float32) / S
    ).astype(jnp.bfloat16)
    outer_flat = outer.reshape(first * second, chans * chans)
    grad_flat = cotangent.reshape(first * second, cotangent.shape[2])
    contract = (((0,), (0,)), ((), ()))
    partial_w = lax.dot_general(outer_flat, grad_flat, contract, preferred_element_type=jnp.float32)
    own_rows = lax.psum_scatter(partial_w, "row", scatter_dimension=0, tiled=True)
    grad_weight = lax.psum(own_rows, "col")
    grad_outer = lax.dot_general(
        grad_flat, weight, (((1,), (1,)), ((), ())), preferred_element_type=jnp.float32
    )
    grad_outer = grad_outer.astype(jnp.bfloat16).reshape(first, second, chans, chans)
    left_part = (
        jnp.einsum("ijcd,dsj->csi", grad_outer, right, preferred_element_type=jnp.float32) / S
    )
    right_part = (
        jnp.einsum("ijcd,csi->dsj", grad_outer, left, preferred_element_type=jnp.float32) / S
    )
    grad_left = lax.psum_scatter(left_part, "col", scatter_dimension=1, tiled=True)
    grad_right = lax.psum_scatter(right_part, "row", scatter_dimension=1, tiled=True)
    return (grad_left, grad_right, grad_weight)


def solution(mesh):
    return jax.shard_map(
        body,
        mesh=mesh,
        in_specs=(P(None, "col", "row"), P(None, "row", "col"), P("row", "col", None), P()),
        out_specs=(P(None, "col", "row"), P(None, "row", "col"), P("row", None)),
        check_vma=False,
    )
```

profile of v0, /device:TPU:0, one launch (start us, length us, event | category | flops | bytes accessed | tf_op | source)
XLA Modules:
  0.0 213.5 jit_solution(4263041880610660756)
XLA Ops:
  7.2 0.0 reduce-scatter.8.cloned.1.call-start
  7.2 17.7 %all_gather.7 = bf16[32,64,32]{2,1,0:T(8,128)(2,1)S(1)} all-gather(bf16[32,16,32]{2,1,0:T(8,128)(2,1)} %param.4), channel_id=1, replica_groups=mesh['row'=8,'col'=4] {'col'}, dimensions={1}, use_global_device_ids=true | all-gather | bytes 163840 | tf_op jit(solution)/shard_map/all_gather | solution.py:10
  24.9 10.3 %all_gather.6 = bf16[32,64,64]{2,1,0:T(8,128)(2,1)S(1)} all-gather(bf16[32,8,64]{2,1,0:T(8,128)(2,1)} %param.5), channel_id=1, replica_groups=mesh['row'=8,'col'=4] {'row'}, dimensions={1}, use_global_device_ids=true | all-gather | bytes 294912 | tf_op jit(solution)/shard_map/all_gather | solution.py:11
  35.2 5.6 %fusion = bf16[32,64,32,32]{1,0,2,3:T(8,128)(2,1)} fusion(bf16[32,64,64]{2,1,0:T(8,128)(2,1)S(1)} %all_gather.6, bf16[32,64,32]{2,1,0:T(8,128)(2,1)S(1)} %all_gather.7), kind=kOutput, calls=%fused_computation.1 | convolution fusion | flops 272629760 | bytes 4587520 | tf_op jit(solution)/shard_map/csi,dsj->ijcd/dot_general | solution.py:15
  40.8 9.1 %copy.20 = bf16[32,64,32,32]{1,0,3,2:T(8,128)(2,1)} copy(bf16[32,64,32,32]{1,0,2,3:T(8,128)(2,1)} %fusion) | data formatting | bytes 8388608 | tf_op jit(solution)/shard_map/convert_element_type | solution.py:16
  49.9 12.4 %reshape.17 = bf16[2048,1024]{0,1:T(8,128)(2,1)} reshape(bf16[32,64,32,32]{1,0,3,2:T(8,128)(2,1)} %copy.20) | data formatting | bytes 8388608 | tf_op jit(solution)/shard_map/reshape | solution.py:17
  62.3 4.3 %fusion.9 = f32[1024,128]{1,0:T(8,128)} fusion(bf16[2048,1024]{0,1:T(8,128)(2,1)} %reshape.17, bf16[2048,128]{1,0:T(8,128)(2,1)S(1)} %bitcast.47), kind=kOutput, calls=%fused_computation.13 | convolution fusion | flops 536870912 | bytes 5242880 | tf_op jit(solution)/shard_map/dot_general | solution.py:20
  66.6 0.0 reduce-scatter.4.cloned.1.call-start
  66.7 3.2 %convolution_convert_fusion = bf16[2048,1024]{1,0:T(8,128)(2,1)} fusion(bf16[2048,128]{1,0:T(8,128)(2,1)S(1)} %bitcast.46, bf16[1024,128]{1,0:T(8,128)(2,1)S(1)} %copy-done.1), kind=kOutput, calls=%fused_computation.2 | convolution fusion | flops 538968064 | bytes 4980736 | tf_op jit(solution)/shard_map/dot_general | solution.py:23
  69.8 6.5 %copy.17 = bf16[2048,1024]{0,1:T(8,128)(2,1)} copy(bf16[2048,1024]{1,0:T(8,128)(2,1)} %convolution_convert_fusion) | data formatting | bytes 8388608 | tf_op jit(solution)/shard_map/convert_element_type | solution.py:26
  76.3 12.9 %reshape.16 = bf16[32,64,32,32]{1,0,3,2:T(8,128)(2,1)} reshape(bf16[2048,1024]{0,1:T(8,128)(2,1)} %copy.17) | data formatting | bytes 8388608 | tf_op jit(solution)/shard_map/reshape | solution.py:26
  89.2 5.7 %fusion.4 = f32[32,64,32]{1,2,0:T(8,128)S(1)} fusion(bf16[32,64,32,32]{1,0,3,2:T(8,128)(2,1)} %reshape.16, bf16[32,64,64]{2,1,0:T(8,128)(2,1)S(1)} %all_gather.6), kind=kOutput, calls=%fused_computation.8 | convolution fusion | flops 268500992 | bytes 4718592 | tf_op jit(solution)/shard_map/ijcd,dsj->csi/dot_general | solution.py:28
  95.0 1.8 copy.18
  96.8 0.2 reduce-scatter.6.cloned.1.call-start
  97.1 7.0 %fusion.2 = f32[32,64,64]{1,2,0:T(8,128)S(1)} fusion(bf16[32,64,32,32]{1,0,3,2:T(8,128)(2,1)} %reshape.16, bf16[32,64,32]{2,1,0:T(8,128)(2,1)S(1)} %all_gather.7), kind=kOutput, calls=%fused_computation.5 | convolution fusion | flops 268566528 | bytes 4849664 | tf_op jit(solution)/shard_map/ijcd,csi->dsj/dot_general | solution.py:31
  104.1 1.8 copy.19
  105.9 0.0 all-reduce.2.cloned.1.call-start
  106.0 0.5 all-reduce.2.cloned.1.call-update
  106.5 24.8 %reduce-scatter.4.cloned.1.call-done = f32[32,16,32]{2,0,1:T(8,128)} async-done(((f32[32,64,32]{2,0,1:T(8,128)}), f32[32,16,32]{2,0,1:T(8,128)}) %reduce-scatter.4.cloned.1.call-update) | async-done | bytes 65552 | tf_op jit(solution)/shard_map/reduce_scatter | solution.py:33
  131.3 1.8 copy.21
  133.1 35.9 %reduce-scatter.6.cloned.1.call-done = f32[32,8,64]{2,0,1:T(8,128)} async-done(((f32[32,64,64]{2,0,1:T(8,128)}), f32[32,8,64]{2,0,1:T(8,128)}) %reduce-scatter.6.cloned.1.call-update) | async-done | bytes 65552 | tf_op jit(solution)/shard_map/reduce_scatter | solution.py:34
  169.0 1.6 copy.22
  170.6 34.9 %all-reduce.2.cloned.1.call-done = f32[128,128]{1,0:T(8,128)} async-done(((f32[128,128]{1,0:T(8,128)}), f32[128,128]{1,0:T(8,128)}) %all-reduce.2.cloned.1.call-update) | async-done | bytes 65552 | tf_op jit(solution)/shard_map/psum | solution.py:22
  205.5 1.5 copy.27
  (8 shorter events, 0.1 us)
Async XLA Ops:
  7.2 55.2 %copy-start = (bf16[32,64,128]{2,1,0:T(8,128)(2,1)S(1)}, bf16[32,64,128]{2,1,0:T(8,128)(2,1)}, u32[]{:S(2)}) copy-start(bf16[32,64,128]{2,1,0:T(8,128)(2,1)} %param.6) | copy-start | bytes 1572868
  7.2 98.8 %reduce-scatter.8.cloned.1.call-start = ((), (), s32[]{:S(2)}) async-start(), calls=%async_computation.5 | async-start | bytes 589824 | tf_op jit(solution)/shard_map/reduce_scatter | solution.py:21
  49.9 16.7 %copy-start.1 = (bf16[1024,128]{1,0:T(8,128)(2,1)S(1)}, bf16[1024,128]{1,0:T(8,128)(2,1)}, u32[]{:S(2)}) copy-start(bf16[1024,128]{1,0:T(8,128)(2,1)} %param.7) | copy-start | bytes 786436
  66.6 64.7 %reduce-scatter.4.cloned.1.call-start = ((), (), s32[]{:S(2)}) async-start(), calls=%async_computation.3 | async-start | bytes 1310720 | tf_op jit(solution)/shard_map/reduce_scatter | solution.py:33
  96.8 72.1 %reduce-scatter.6.cloned.1.call-start = ((), (), s32[]{:S(2)}) async-start(), calls=%async_computation.4 | async-start | bytes 1179648 | tf_op jit(solution)/shard_map/reduce_scatter | solution.py:34
  105.9 99.6 %all-reduce.2.cloned.1.call-start = ((), (), s32[]{:S(2)}) async-start(), calls=%async_computation.6 | async-start | bytes 131072 | tf_op jit(solution)/shard_map/psum | solution.py:22
Sparse Core Ops, SparseCore 0:
  66.7 34.8 reduce-scatter.7
  103.9 27.3 reduce-scatter.3
  134.5 34.4 reduce-scatter.5
  171.1 34.2 all-reduce.1
where the time goes:
time: 215 us; the launch traced here: 213 us
  waiting for transfers between devices  96.1 us (45%)
  local copies, waits for them, and re-layouts  49.4 us (23%)
  blocking collectives  28 us (13%)
  matrix products  25.8 us (12%)
  between operations  13.8 us (6%)
    reduce_scatter x1, waiting for transfers between devices, body(): lax.psum_scatter(right_part, 'row', scatter_dimension=1, tiled=True)  35.9 us
    psum x1, waiting for transfers between devices, body(): grad_weight = lax.psum(own_rows, 'col')  34.9 us
    reduce_scatter x1, waiting for transfers between devices, body(): lax.psum_scatter(left_part, 'col', scatter_dimension=1, tiled=True)  24.8 us
    all_gather x1, blocking collectives, body(): left = lax.all_gather(left_act, 'col', axis=1, tiled=True)  17.7 us
    reshape x1, local copies, waits for them, and re-layouts, body(): grad_outer.astype(jnp.bfloat16).reshape(first, second, chans, chans)  12.9 us
    reshape x1, local copies, waits for them, and re-layouts, body(): outer_flat = outer.reshape(first * second, chans * chans)  12.4 us
    all_gather x1, blocking collectives, body(): right = lax.all_gather(right_act, 'row', axis=1, tiled=True)  10.3 us
    convert_element_type x1, local copies, waits for them, and re-layouts, body(): outer = (jnp.einsum('csi,dsj->ijcd', left, right, preferred_element_type=...  9.13 us
  transfers between devices with their start and end apart: 4, of which 3 were waited for; matrix products, arithmetic and copies ran while one was open for 20% of the time, Pallas kernels for 0%

commit v1 on v0

--- a/solution.py
+++ b/solution.py
@@ -19,7 +19,8 @@
     contract = (((0,), (0,)), ((), ()))
     partial_w = lax.dot_general(outer_flat, grad_flat, contract, preferred_element_type=jnp.float32)
     own_rows = lax.psum_scatter(partial_w, "row", scatter_dimension=0, tiled=True)
-    grad_weight = lax.psum(own_rows, "col")
+    blocks = lax.all_gather(own_rows, "col", axis=0, tiled=False)
+    grad_weight = blocks.sum(axis=0)
     grad_outer = lax.dot_general(
         grad_flat, weight, (((1,), (1,)), ((), ())), preferred_element_type=jnp.float32
     )

time: 215 us -> 185 us (0.86)
  waiting for transfers between devices: 96.1 us -> 46.6 us
  blocking collectives: 28 us -> 48.2 us
    psum x1 -> x0, waiting for transfers between devices: 34.9 us -> none  [body(): grad_weight = lax.psum(own_rows, 'col')]
    reduce_scatter x1, waiting for transfers between devices: 24.8 us -> 0.02 us  [body(): lax.psum_scatter(left_part, 'col', scatter_dimension=1, tiled=True)]
    reduce_scatter x1, waiting for transfers between devices: 0.02 us -> 22.1 us  [body(): lax.psum_scatter(partial_w, 'row', scatter_dimension=0, tiled=True)]
    all_gather x0 -> x1, blocking collectives: none -> 14.1 us  [body(): blocks = lax.all_gather(own_rows, 'col', axis=0, tiled=False)]
    reduce_scatter x1, waiting for transfers between devices: 35.9 us -> 24.4 us  [body(): lax.psum_scatter(right_part, 'row', scatter_dimension=1, tiled=True)]
    all_gather x1, blocking collectives: 17.7 us -> 22.2 us  [body(): left = lax.all_gather(left_act, 'col', axis=1, tiled=True)]
    unnamed x7 -> x6, local copies, waits for them, and re-layouts: 4.93 us -> 3.47 us
  transfers between devices with their start and end apart: 4 -> 3, of which waited for: 3 -> 2; matrix products, arithmetic and copies ran while one was open for 20% -> 23% of each run, Pallas kernels for 0% -> 0%
where the time goes in v1:
time: 185 us; the launch traced here: 184 us
  blocking collectives  48.2 us (26%)
  local copies, waits for them, and re-layouts  47.9 us (26%)
  waiting for transfers between devices  46.6 us (25%)
  matrix products  26.7 us (14%)
  between operations  13.8 us (7%)
    reduce_scatter x1, waiting for transfers between devices, body(): lax.psum_scatter(right_part, 'row', scatter_dimension=1, tiled=True)  24.4 us
    all_gather x1, blocking collectives, body(): left = lax.all_gather(left_act, 'col', axis=1, tiled=True)  22.2 us
    reduce_scatter x1, waiting for transfers between devices, body(): lax.psum_scatter(partial_w, 'row', scatter_dimension=0, tiled=True)  22.1 us
    all_gather x1, blocking collectives, body(): blocks = lax.all_gather(own_rows, 'col', axis=0, tiled=False)  14.1 us
    reshape x1, local copies, waits for them, and re-layouts, body(): grad_outer.astype(jnp.bfloat16).reshape(first, second, chans, chans)  12.9 us
    reshape x1, local copies, waits for them, and re-layouts, body(): outer_flat = outer.reshape(first * second, chans * chans)  12.3 us
    all_gather x1, blocking collectives, body(): right = lax.all_gather(right_act, 'row', axis=1, tiled=True)  11.9 us
    convert_element_type x1, local copies, waits for them, and re-layouts, body(): outer = (jnp.einsum('csi,dsj->ijcd', left, right, preferred_element_type=...  9.17 us
  transfers between devices with their start and end apart: 3, of which 2 were waited for; matrix products, arithmetic and copies ran while one was open for 23% of the time, Pallas kernels for 0%

profile of v1, /device:TPU:0, one launch (start us, length us, event | category | flops | bytes accessed | tf_op | source)
XLA Modules:
  0.0 184.1 jit_solution(14907400142397622416)
XLA Ops:
  7.2 0.0 reduce-scatter.4.cloned.1.call-start
  7.2 11.9 %all_gather.12 = bf16[32,64,64]{2,1,0:T(8,128)(2,1)S(1)} all-gather(bf16[32,8,64]{2,1,0:T(8,128)(2,1)} %param.5), channel_id=1, replica_groups=mesh['row'=8,'col'=4] {'row'}, dimensions={1}, use_global_device_ids=true | all-gather | bytes 294912 | tf_op jit(solution)/shard_map/all_gather | solution.py:11
  19.1 4.1 %convolution_convert_fusion = bf16[2048,1024]{1,0:T(8,128)(2,1)} fusion(bf16[2048,128]{1,0:T(8,128)(2,1)S(1)} %bitcast.47, bf16[1024,128]{1,0:T(8,128)(2,1)} %param.7), kind=kOutput, calls=%fused_computation.2 | convolution fusion | flops 538968064 | bytes 4980736 | tf_op jit(solution)/shard_map/dot_general | solution.py:24
  23.2 6.5 %copy.17 = bf16[2048,1024]{0,1:T(8,128)(2,1)} copy(bf16[2048,1024]{1,0:T(8,128)(2,1)} %convolution_convert_fusion) | data formatting | bytes 8388608 | tf_op jit(solution)/shard_map/convert_element_type | solution.py:27
  29.7 12.9 %reshape.16 = bf16[32,64,32,32]{1,0,3,2:T(8,128)(2,1)} reshape(bf16[2048,1024]{0,1:T(8,128)(2,1)} %copy.17) | data formatting | bytes 8388608 | tf_op jit(solution)/shard_map/reshape | solution.py:27
  42.6 5.7 %fusion.4 = f32[32,64,32]{1,2,0:T(8,128)S(1)} fusion(bf16[32,64,32,32]{1,0,3,2:T(8,128)(2,1)} %reshape.16, bf16[32,64,64]{2,1,0:T(8,128)(2,1)S(1)} %all_gather.12), kind=kOutput, calls=%fused_computation.8 | convolution fusion | flops 268500992 | bytes 4718592 | tf_op jit(solution)/shard_map/ijcd,dsj->csi/dot_general | solution.py:29
  48.3 1.9 %copy.18 = f32[32,64,32]{2,0,1:T(8,128)} copy(f32[32,64,32]{1,2,0:T(8,128)S(1)} %fusion.4) | data formatting | bytes 524288 | tf_op jit(solution)/shard_map/div | solution.py:29
  50.2 0.0 reduce-scatter.4.cloned.1.call-update
  50.2 0.0 reduce-scatter.8.cloned.1.call-start
  50.2 22.2 %all_gather.13 = bf16[32,64,32]{2,1,0:T(8,128)(2,1)S(1)} all-gather(bf16[32,16,32]{2,1,0:T(8,128)(2,1)S(1)} %copy-done.1), channel_id=1, replica_groups=mesh['row'=8,'col'=4] {'col'}, dimensions={1}, use_global_device_ids=true | all-gather | bytes 163840 | tf_op jit(solution)/shard_map/all_gather | solution.py:10
  72.4 5.6 %fusion = bf16[32,64,32,32]{1,0,2,3:T(8,128)(2,1)} fusion(bf16[32,64,64]{2,1,0:T(8,128)(2,1)S(1)} %all_gather.12, bf16[32,64,32]{2,1,0:T(8,128)(2,1)S(1)} %all_gather.13), kind=kOutput, calls=%fused_computation.1 | convolution fusion | flops 272629760 | bytes 4587520 | tf_op jit(solution)/shard_map/csi,dsj->ijcd/dot_general | solution.py:15
  78.0 9.2 %copy.20 = bf16[32,64,32,32]{1,0,3,2:T(8,128)(2,1)} copy(bf16[32,64,32,32]{1,0,2,3:T(8,128)(2,1)} %fusion) | data formatting | bytes 8388608 | tf_op jit(solution)/shard_map/convert_element_type | solution.py:16
  87.2 12.3 %reshape.17 = bf16[2048,1024]{0,1:T(8,128)(2,1)} reshape(bf16[32,64,32,32]{1,0,3,2:T(8,128)(2,1)} %copy.20) | data formatting | bytes 8388608 | tf_op jit(solution)/shard_map/reshape | solution.py:17
  99.5 4.2 %fusion.9 = f32[1024,128]{1,0:T(8,128)} fusion(bf16[2048,1024]{0,1:T(8,128)(2,1)} %reshape.17, bf16[2048,128]{1,0:T(8,128)(2,1)S(1)} %bitcast.48), kind=kOutput, calls=%fused_computation.13 | convolution fusion | flops 536870912 | bytes 5242880 | tf_op jit(solution)/shard_map/dot_general | solution.py:20
  103.8 0.2 reduce-scatter.6.cloned.1.call-start
  104.0 7.0 %fusion.2 = f32[32,64,64]{1,2,0:T(8,128)S(1)} fusion(bf16[32,64,32,32]{1,0,3,2:T(8,128)(2,1)} %reshape.16, bf16[32,64,32]{2,1,0:T(8,128)(2,1)S(1)} %all_gather.13), kind=kOutput, calls=%fused_computation.5 | convolution fusion | flops 268566528 | bytes 4849664 | tf_op jit(solution)/shard_map/ijcd,csi->dsj/dot_general | solution.py:32
  111.1 1.8 copy.19
  112.9 0.0 reduce-scatter.4.cloned.1.call-done
  112.9 1.8 copy.21
  114.7 22.1 %reduce-scatter.8.cloned.1.call-done = f32[128,128]{1,0:T(8,128)} async-done(((f32[1024,128]{1,0:T(8,128)}), f32[128,128]{1,0:T(8,128)}) %reduce-scatter.8.cloned.1.call-update) | async-done | bytes 65552 | tf_op jit(solution)/shard_map/reduce_scatter | solution.py:21
  136.8 14.1 %all-gather = f32[512,128]{1,0:T(8,128)S(1)} all-gather(f32[128,128]{1,0:T(8,128)} %reduce-scatter.8.cloned.1.call-done), channel_id=2, replica_groups=mesh['row'=8,'col'=4] {'col'}, dimensions={0}, use_global_device_ids=true | all-gather | bytes 327680 | tf_op jit(solution)/shard_map/all_gather | solution.py:22
  150.9 0.6 reduce_sum.9
  151.5 24.4 %reduce-scatter.6.cloned.1.call-done = f32[32,8,64]{2,0,1:T(8,128)} async-done(((f32[32,64,64]{2,0,1:T(8,128)}), f32[32,8,64]{2,0,1:T(8,128)}) %reduce-scatter.6.cloned.1.call-update) | async-done | bytes 65552 | tf_op jit(solution)/shard_map/reduce_scatter | solution.py:35
  176.0 1.6 copy.22
  (6 shorter events, 0.0 us)
Async XLA Ops:
  7.2 12.0 %copy-start = (bf16[32,64,128]{2,1,0:T(8,128)(2,1)S(1)}, bf16[32,64,128]{2,1,0:T(8,128)(2,1)}, u32[]{:S(2)}) copy-start(bf16[32,64,128]{2,1,0:T(8,128)(2,1)} %param.6) | copy-start | bytes 1572868
  7.2 105.7 %reduce-scatter.4.cloned.1.call-start = ((), (), s32[]{:S(2)}) async-start(), calls=%async_computation.3 | async-start | bytes 1310720 | tf_op jit(solution)/shard_map/reduce_scatter | solution.py:34
  42.6 7.7 %copy-start.1 = (bf16[32,16,32]{2,1,0:T(8,128)(2,1)S(1)}, bf16[32,16,32]{2,1,0:T(8,128)(2,1)}, u32[]{:S(2)}) copy-start(bf16[32,16,32]{2,1,0:T(8,128)(2,1)} %param.4) | copy-start | bytes 98308
  50.2 86.6 %reduce-scatter.8.cloned.1.call-start = ((), (), s32[]{:S(2)}) async-start(), calls=%async_computation.5 | async-start | bytes 589824 | tf_op jit(solution)/shard_map/reduce_scatter | solution.py:21
  103.8 72.2 %reduce-scatter.6.cloned.1.call-start = ((), (), s32[]{:S(2)}) async-start(), calls=%async_computation.4 | async-start | bytes 1179648 | tf_op jit(solution)/shard_map/reduce_scatter | solution.py:35
Sparse Core Ops, SparseCore 0:
  50.3 32.7 reduce-scatter.3
  103.9 32.8 reduce-scatter.7
  139.9 35.9 reduce-scatter.5
